TPU v7x, 32 devices: a whole 2x2x4 slice. The times are simulated.
32 devices in a mesh: mem: 8 (over z, y), lat: 4 (over x, core).
Axes of the slice: x: 2, y: 2, z: 4, core: 2. Of those that a mesh axis runs over, the one named last changes fastest.
Arguments:
- prior_sample_states: bfloat16 [16, 2, 16, 1024], P('mem', None, 'lat'), may hold values from -6 to 6
- wind_cfl_ratios: float32 [2, 16, 1024], P(None, 'lat'), may hold values from -0.45 to 0.45
- obs_cell: int32 [4, 2048], P('lat', 'mem'), may hold values from 0 to 511
- obs_value: float32 [4, 2048], P('lat', 'mem'), may hold values from -6 to 6
- obs_precision: float32 [4, 2048], P('lat', 'mem'), may hold values from 0.25 to 4
- neighbours: int32 [16, 8, 512], P('lat', 'mem'), may hold values from 0 to 1279, as said below
- obs_counts: int32 [16, 8], P('lat', 'mem'), may hold values from 128 to 512, as said below
Outputs:
- analysis: bfloat16 [16, 2, 16, 1024], P('mem', None, 'lat')
Inputs may be any that keep to these rules, and one draw needn't show every extreme that they name: `obs_counts`: in every tile some block's list has all 512 slots live. `neighbours`: the 512 entries of one list are distinct and index the extended set of its tile.
All inputs are finite; a program needn't handle non-finite values. Where the computation divides by a largest or mean magnitude, that divisor is 1e-20 or more.
Results may differ from a plain program's by a relative error of at most 0.0053.
Values may be sent and summed in bfloat16 or wider, within the bound.
A program may use at most 64 MiB of HBM per device.

v0:
```python
import jax
import jax.numpy as jnp
from jax import lax
from jax.sharding import PartitionSpec as P

PATCH_WIDTH = 128
SECTIONS = 4
NS_ITERS = 6
LOC_ROWS = 2
LOC_COLS = 64
KAPPA = (0.025, 0.0125)
HIGHEST = lax.Precision.HIGHEST


def with_halo(cells, sides, width):
    for axis, dim in sides:
        count = lax.axis_size(axis)
        ends = count - 1
        head = lax.slice_in_dim(cells, 0, width, axis=dim)
        tail = lax.slice_in_dim(cells, cells.shape[dim] - width, cells.shape[dim], axis=dim)
        cells = jnp.concatenate(
            [
                lax.ppermute(tail, axis, [(i, (i + 1) % count) for i in range(ends)]),
                cells,
                lax.ppermute(head, axis, [((i + 1) % count, i) for i in range(ends)]),
            ],
            axis=dim,
        )
    return cells


def advance(padded, east_wind, north_wind, diffusion):
    centre = padded[:, 1:-1, :]
    north_row = padded[:, 2:, :]
    south_row = padded[:, :-2, :]
    widened = jnp.pad(centre, ((0, 0), (0, 0), (1, 1)))
    west_cell = widened[:, :, :-2]
    east_cell = widened[:, :, 2:]
    transport = (
        jnp.maximum(east_wind, 0.0) * (centre - west_cell)
        + jnp.minimum(east_wind, 0.0) * (east_cell - centre)
        + jnp.maximum(north_wind, 0.0) * (centre - south_row)
        + jnp.minimum(north_wind, 0.0) * (north_row - centre)
    )
    return (
        centre
        - transport
        + diffusion * (north_row + south_row + east_cell + west_cell - 4.0 * centre)
    )


def place_piece(piece, sample_realizations, row_shift, col_shift):
    return jnp.concatenate(
        [
            piece[: sample_realizations + 2],
            piece[sample_realizations + 2 : sample_realizations + 3] + row_shift,
            piece[sample_realizations + 3 :] + col_shift,
        ],
        axis=0,
    )


def analyze(mesh_patch, extended, block_lists, block_counts):
    sample_realizations = mesh_patch.shape[0]
    analysis_block_count = mesh_patch.shape[2]
    tile_width = mesh_patch.shape[3]
    extent = extended.shape[1]
    slot_count = block_lists.shape[1]
    obs_ens = extended[:sample_realizations]
    obs_mean = jnp.mean(obs_ens, axis=0)
    spread = obs_ens - obs_mean
    innovation = extended[sample_realizations] - obs_mean
    precision = extended[sample_realizations + 1]
    obs_row = extended[sample_realizations + 2]
    obs_col = extended[sample_realizations + 3]
    active = (jnp.arange(slot_count, dtype=jnp.int32)[None, :] < block_counts[:, None]).astype(
        jnp.float32
    )
    block_ids = jnp.broadcast_to(
        jnp.arange(analysis_block_count, dtype=jnp.int32)[:, None], block_lists.shape
    )
    membership = (
        jnp.zeros((analysis_block_count, extent), jnp.float32)
        .at[block_ids, block_lists]
        .set(active)
    )
    block_row = jnp.arange(analysis_block_count, dtype=jnp.float32)[:, None]
    row_gap = obs_row[None, :] - block_row
    col_gap = obs_col[None, :] - 0.5 * (tile_width - 1)
    tapering = jnp.exp(-0.5 * ((row_gap / LOC_ROWS) ** 2 + (col_gap / LOC_COLS) ** 2))
    weight = membership * tapering * precision[None, :]
    weighted = spread[None, :, :] * weight[:, None, :]
    gram_matrix = jnp.einsum("rek,fk->ref", weighted, spread, precision=HIGHEST)
    forcing = jnp.einsum("ek,rk->re", spread, weight * innovation[None, :], precision=HIGHEST)
    identity = jnp.eye(sample_realizations, dtype=jnp.float32)
    system = (sample_realizations - 1.0) * identity + gram_matrix
    bounds = sample_realizations - 1.0 + jnp.max(jnp.sum(jnp.abs(gram_matrix), axis=2), axis=1)
    upper_iter = system / bounds[:, None, None]
    lower_iter = jnp.broadcast_to(identity, system.shape)
    for iteration in range(NS_ITERS):
        factor = 1.5 * identity - 0.5 * jnp.einsum(
            "rij,rjk->rik", lower_iter, upper_iter, precision=HIGHEST
        )
        upper_iter = jnp.einsum("rij,rjk->rik", upper_iter, factor, precision=HIGHEST)
        lower_iter = jnp.einsum("rij,rjk->rik", factor, lower_iter, precision=HIGHEST)
    inv_root = lower_iter / jnp.sqrt(bounds)[:, None, None]
    half_shift = jnp.einsum("rij,rj->ri", inv_root, forcing, precision=HIGHEST)
    mean_shift = jnp.einsum("rij,rj->ri", inv_root, half_shift, precision=HIGHEST)
    weights = jnp.sqrt(sample_realizations - 1.0) * inv_root + mean_shift[:, :, None]
    fields = mesh_patch.astype(jnp.float32)
    centre = jnp.mean(fields, axis=0)
    anomalies = fields - centre
    updated = centre + jnp.einsum("kvrc,rkm->mvrc", anomalies, weights, precision=HIGHEST)
    return updated.astype(jnp.bfloat16)


def on_device(
    prior_sample_states, wind_cfl_ratios, obs_cell, obs_value, obs_precision, neighbours, obs_counts
):
    ensemble_count = prior_sample_states.shape[0]
    analysis_block_count = prior_sample_states.shape[2]
    longitude_index = prior_sample_states.shape[3]
    present_states = prior_sample_states.astype(jnp.float32).reshape(
        ensemble_count * 2, analysis_block_count, longitude_index
    )
    diffusion = jnp.tile(jnp.array(KAPPA, jnp.float32).reshape(2, 1, 1), (ensemble_count, 1, 1))
    for section_index in range(SECTIONS):
        padded = with_halo(present_states, (("lat", 1),), 1)
        present_states = advance(padded, wind_cfl_ratios[0], wind_cfl_ratios[1], diffusion)
    predict_advance = present_states.astype(jnp.bfloat16).reshape(
        ensemble_count, 2, analysis_block_count, longitude_index
    )
    cells = obs_cell[0]
    own_meta = jnp.stack(
        [
            obs_value[0],
            obs_precision[0],
            (cells // PATCH_WIDTH).astype(jnp.float32),
            (cells % PATCH_WIDTH).astype(jnp.float32),
        ],
        axis=0,
    )
    mesh_patches = lax.all_to_all(predict_advance, "mem", split_axis=3, concat_axis=0, tiled=True)
    sample_realizations = mesh_patches.shape[0]
    own_obs = jnp.take(mesh_patches[:, 0].reshape(sample_realizations, -1), cells, axis=1).astype(
        jnp.float32
    )
    combined = jnp.concatenate([own_obs, own_meta], axis=0)
    beside_all = with_halo(combined[None, None], (("mem", 1), ("lat", 0)), 1)
    pieces = [
        beside_all[1, 1],
        beside_all[0, 1],
        beside_all[2, 1],
        beside_all[1, 0],
        beside_all[1, 2],
    ]
    row_span = float(analysis_block_count)
    col_span = float(PATCH_WIDTH)
    shifts = [(0.0, 0.0), (-row_span, 0.0), (row_span, 0.0), (0.0, -col_span), (0.0, col_span)]
    extended = jnp.concatenate(
        [
            place_piece(pieces[slot], sample_realizations, shifts[slot][0], shifts[slot][1])
            for slot in range(5)
        ],
        axis=1,
    )
    updated = analyze(mesh_patches, extended, neighbours[:, 0, :], obs_counts[:, 0])
    return lax.all_to_all(updated, "mem", split_axis=0, concat_axis=3, tiled=True)


def solution(mesh):
    placed = (
        P("mem", None, "lat", None),
        P(None, "lat", None),
        P("lat", "mem"),
        P("lat", "mem"),
        P("lat", "mem"),
        P("lat", "mem", None),
        P("lat", "mem"),
    )
    return jax.shard_map(
        on_device,
        mesh=mesh,
        in_specs=placed,
        out_specs=P("mem", None, "lat", None),
        check_vma=False,
    )
```

profile of v0, /device:TPU:1, one launch (start us, length us, event | category | flops | bytes accessed | tf_op | source)
XLA Modules:
  0.0 93.3 jit_solution(944328057822813094)
XLA Ops:
  0.0 0.8 bitcast_convert_fusion
  0.8 4.5 %collective-permute-start = (f32[4,1,1024]{2,0,1:T(4,128)S(1)}, f32[4,1,1024]{2,0,1:T(4,128)S(1)}, u32[]{:S(2)}, u32[]{:S(2)}) collective-permute-start(f32[4,1,1024]{2,0,1:T(4,128)S(1)} %get-tuple-element.17), channel_id=1, source_target_pairs={{0,1},{1,2},{2,3},{4,5},{5,6},{6,7},{8,9},{9,10},{10,11},{12,13},{... | collective-permute-start | bytes 49160 | tf_op jit(solution)/shard_map/ppermute | solution.py:23
  5.4 1.9 %collective-permute-start.1 = (f32[4,1,1024]{2,0,1:T(4,128)S(1)}, f32[4,1,1024]{2,0,1:T(4,128)S(1)}, u32[]{:S(2)}, u32[]{:S(2)}) collective-permute-start(f32[4,1,1024]{2,0,1:T(4,128)S(1)} %get-tuple-element.18), channel_id=1, source_target_pairs={{1,0},{2,1},{3,2},{5,4},{6,5},{7,6},{9,8},{10,9},{11,10},{13,12},{... | collective-permute-start | bytes 49160 | tf_op jit(solution)/shard_map/ppermute | solution.py:25
  7.4 0.6 copy-done.2
  8.1 0.6 copy-done.6
  8.8 0.6 copy-done.7
  9.5 0.6 copy-done.5
  10.2 0.6 copy-done.8
  11.1 3.6 %collective-permute-start.2 = (f32[4,1,1024]{2,0,1:T(4,128)S(1)}, f32[4,1,1024]{2,0,1:T(4,128)S(1)}, u32[]{:S(2)}, u32[]{:S(2)}) collective-permute-start(f32[4,1,1024]{2,0,1:T(4,128)S(1)} %get-tuple-element.15), channel_id=1, source_target_pairs={{0,1},{1,2},{2,3},{4,5},{5,6},{6,7},{8,9},{9,10},{10,11},{12,13},{... | collective-permute-start | bytes 49160 | tf_op jit(solution)/shard_map/ppermute | solution.py:23
  14.8 1.9 %collective-permute-start.3 = (f32[4,1,1024]{2,0,1:T(4,128)S(1)}, f32[4,1,1024]{2,0,1:T(4,128)S(1)}, u32[]{:S(2)}, u32[]{:S(2)}) collective-permute-start(f32[4,1,1024]{2,0,1:T(4,128)S(1)} %get-tuple-element.16), channel_id=1, source_target_pairs={{1,0},{2,1},{3,2},{5,4},{6,5},{7,6},{9,8},{10,9},{11,10},{13,12},{... | collective-permute-start | bytes 49160 | tf_op jit(solution)/shard_map/ppermute | solution.py:25
  16.7 3.1 %collective-permute-done.3 = f32[4,1,1024]{2,0,1:T(4,128)S(1)} collective-permute-done((f32[4,1,1024]{2,0,1:T(4,128)S(1)}, f32[4,1,1024]{2,0,1:T(4,128)S(1)}, u32[]{:S(2)}, u32[]{:S(2)}) %collective-permute-start.3) | collective-permute-done | bytes 16416 | tf_op jit(solution)/shard_map/ppermute | solution.py:25
  20.0 1.9 %collective-permute-start.4 = (f32[4,1,1024]{2,0,1:T(4,128)S(1)}, f32[4,1,1024]{2,0,1:T(4,128)S(1)}, u32[]{:S(2)}, u32[]{:S(2)}) collective-permute-start(f32[4,1,1024]{2,0,1:T(4,128)S(1)} %get-tuple-element.13), channel_id=1, source_target_pairs={{0,1},{1,2},{2,3},{4,5},{5,6},{6,7},{8,9},{9,10},{10,11},{12,13},{... | collective-permute-start | bytes 49160 | tf_op jit(solution)/shard_map/ppermute | solution.py:23
  21.9 2.4 %collective-permute-start.5 = (f32[4,1,1024]{2,0,1:T(4,128)S(1)}, f32[4,1,1024]{2,0,1:T(4,128)S(1)}, u32[]{:S(2)}, u32[]{:S(2)}) collective-permute-start(f32[4,1,1024]{2,0,1:T(4,128)S(1)} %get-tuple-element.14), channel_id=1, source_target_pairs={{1,0},{2,1},{3,2},{5,4},{6,5},{7,6},{9,8},{10,9},{11,10},{13,12},{... | collective-permute-start | bytes 49160 | tf_op jit(solution)/shard_map/ppermute | solution.py:25
  24.4 2.6 %collective-permute-done.5 = f32[4,1,1024]{2,0,1:T(4,128)S(1)} collective-permute-done((f32[4,1,1024]{2,0,1:T(4,128)S(1)}, f32[4,1,1024]{2,0,1:T(4,128)S(1)}, u32[]{:S(2)}, u32[]{:S(2)}) %collective-permute-start.5) | collective-permute-done | bytes 16416 | tf_op jit(solution)/shard_map/ppermute | solution.py:25
  27.2 1.9 %collective-permute-start.6 = (f32[4,1,1024]{2,0,1:T(4,128)S(1)}, f32[4,1,1024]{2,0,1:T(4,128)S(1)}, u32[]{:S(2)}, u32[]{:S(2)}) collective-permute-start(f32[4,1,1024]{2,0,1:T(4,128)S(1)} %get-tuple-element.11), channel_id=1, source_target_pairs={{0,1},{1,2},{2,3},{4,5},{5,6},{6,7},{8,9},{9,10},{10,11},{12,13},{... | collective-permute-start | bytes 49160 | tf_op jit(solution)/shard_map/ppermute | solution.py:23
  29.1 2.4 %collective-permute-start.7 = (f32[4,1,1024]{2,0,1:T(4,128)S(1)}, f32[4,1,1024]{2,0,1:T(4,128)S(1)}, u32[]{:S(2)}, u32[]{:S(2)}) collective-permute-start(f32[4,1,1024]{2,0,1:T(4,128)S(1)} %get-tuple-element.12), channel_id=1, source_target_pairs={{1,0},{2,1},{3,2},{5,4},{6,5},{7,6},{9,8},{10,9},{11,10},{13,12},{... | collective-permute-start | bytes 49160 | tf_op jit(solution)/shard_map/ppermute | solution.py:25
  31.5 8.1 %scatter_custom_fusion = f32[5120]{0:T(1024)S(1)} fusion(s32[2048]{0:T(1024)S(1)} %bitcast.143, f32[2048]{0:T(1024)S(1)} %bitcast.144, f32[]{:T(128)} %constant.37.clone.1), kind=kCustom, calls=%fused_computation.134 | custom fusion | bytes 20484
  39.9 0.8 copy.122
  40.7 2.6 %reshape.227 = bf16[8,2,1024]{2,1,0:T(2,128)(2,1)} reshape(bf16[1024,2,2,4]{3,2,1,0:T(2,128)(2,1)S(1)} %bitcast.128) | data formatting | bytes 65536
  43.3 5.6 %all-to-all-start = ((bf16[8,2,1024]{2,1,0:T(2,128)(2,1)}), bf16[8,2,1024]{2,1,0:T(2,128)(2,1)S(1)}, u32[]{:S(2)}, u32[]{:S(2)}) async-start(bf16[8,2,1024]{2,1,0:T(2,128)(2,1)} %reshape.227), calls=%async_computation | async-start | bytes 65536 | tf_op jit(solution)/shard_map/all_to_all | solution.py:143
  48.9 5.6 %all-to-all-done = bf16[8,2,1024]{2,1,0:T(2,128)(2,1)S(1)} async-done(((bf16[8,2,1024]{2,1,0:T(2,128)(2,1)}), bf16[8,2,1024]{2,1,0:T(2,128)(2,1)S(1)}, u32[]{:S(2)}, u32[]{:S(2)}) %all-to-all-start) | async-done | bytes 32800 | tf_op jit(solution)/shard_map/all_to_all | solution.py:143
  54.5 2.2 %reshape.228 = bf16[1024,2,2,4]{3,2,1,0:T(2,128)(2,1)S(1)} reshape(bf16[8,2,1024]{2,1,0:T(2,128)(2,1)S(1)} %all-to-all-done) | data formatting | bytes 65536
  56.7 1.3 %copy.123 = bf16[2,2,4,8,128]{4,3,2,1,0:T(8,128)(2,1)S(1)} copy(bf16[2,2,4,8,128]{2,1,0,4,3:T(2,128)(2,1)S(1)} %bitcast.129) | data formatting | bytes 65536 | tf_op jit(solution)/shard_map/all_to_all | solution.py:143
  58.2 0.9 gather_fusion
  59.2 0.6 copy-done.4
  60.0 2.3 %collective-permute-start.8 = (f32[1,1,20,256]{3,2,1,0:T(8,128)S(1)}, f32[1,1,20,256]{3,2,1,0:T(8,128)S(1)}, u32[]{:S(2)}, u32[]{:S(2)}) collective-permute-start(f32[1,1,20,256]{3,2,1,0:T(8,128)S(1)} %bitcast.132), channel_id=1, source_target_pairs={{0,4},{4,8},{8,12},{12,16},{16,20},{20,24},{24,28},{1,5},{5,9},{9,... | collective-permute-start | bytes 61448 | tf_op jit(solution)/shard_map/ppermute | solution.py:23
  62.3 1.3 %collective-permute-start.9 = (f32[1,1,20,256]{3,2,1,0:T(8,128)S(1)}, f32[1,1,20,256]{3,2,1,0:T(8,128)S(1)}, u32[]{:S(2)}, u32[]{:S(2)}) collective-permute-start(f32[1,1,20,256]{3,2,1,0:T(8,128)S(1)} %bitcast.133), channel_id=1, source_target_pairs={{4,0},{8,4},{12,8},{16,12},{20,16},{24,20},{28,24},{5,1},{9,5},{13... | collective-permute-start | bytes 61448 | tf_op jit(solution)/shard_map/ppermute | solution.py:25
  63.7 3.1 %collective-permute-done.9 = f32[1,1,20,256]{3,2,1,0:T(8,128)S(1)} collective-permute-done((f32[1,1,20,256]{3,2,1,0:T(8,128)S(1)}, f32[1,1,20,256]{3,2,1,0:T(8,128)S(1)}, u32[]{:S(2)}, u32[]{:S(2)}) %collective-permute-start.9) | collective-permute-done | bytes 20512 | tf_op jit(solution)/shard_map/ppermute | solution.py:25
  66.9 5.7 %collective-permute-start.10 = (f32[1,3,20,256]{3,0,2,1:T(1,128)S(1)}, f32[1,3,20,256]{3,0,2,1:T(1,128)S(1)}, u32[]{:S(2)}, u32[]{:S(2)}) collective-permute-start(f32[1,3,20,256]{3,0,2,1:T(1,128)S(1)} %copy_dynamic-update-slice_fusion), channel_id=1, source_target_pairs={{0,1},{1,2},{2,3},{4,5},{5,6},{6,7},{8,9},{9,10},{10,11},{12,13},{... | collective-permute-start | bytes 184328 | tf_op jit(solution)/shard_map/ppermute | solution.py:23
  72.6 1.9 %collective-permute-start.11 = (f32[1,3,20,256]{3,0,2,1:T(1,128)S(1)}, f32[1,3,20,256]{3,0,2,1:T(1,128)S(1)}, u32[]{:S(2)}, u32[]{:S(2)}) collective-permute-start(f32[1,3,20,256]{3,0,2,1:T(1,128)S(1)} %copy_dynamic-update-slice_fusion), channel_id=1, source_target_pairs={{1,0},{2,1},{3,2},{5,4},{6,5},{7,6},{9,8},{10,9},{11,10},{13,12},{... | collective-permute-start | bytes 184328 | tf_op jit(solution)/shard_map/ppermute | solution.py:25
  74.6 3.5 %collective-permute-done.11 = f32[1,3,20,256]{3,0,2,1:T(1,128)S(1)} collective-permute-done((f32[1,3,20,256]{3,0,2,1:T(1,128)S(1)}, f32[1,3,20,256]{3,0,2,1:T(1,128)S(1)}, u32[]{:S(2)}, u32[]{:S(2)}) %collective-permute-start.11) | collective-permute-done | bytes 61472 | tf_op jit(solution)/shard_map/ppermute | solution.py:25
  78.4 1.3 %abs_reduce_fusion = (f32[4,16]{1,0:T(4,128)S(1)}, f32[4,16,16]{1,2,0:T(8,128)S(1)}) fusion(f32[16,1280]{1,0:T(8,128)S(1)} %slice_subtract_fusion, f32[4,1280]{1,0:T(4,128)S(1)} %multiply_multiply_fusion), kind=kOutput, calls=%fused_computation.104 | convolution fusion | flops 15812544 | bytes 106752 | tf_op jit(solution)/shard_map/rek,fk->ref/dot_general | solution.py:93
  79.8 0.3 fusion.7
  80.1 0.3 fusion.97
  80.6 0.2 fusion.6
  80.7 0.2 fusion.103
  81.1 0.2 fusion.5
  81.3 0.2 fusion.105
  81.6 0.2 fusion.4
  82.1 0.2 fusion.3
  82.6 0.2 fusion.72
  82.8 0.2 fusion.2
  83.0 0.2 convolution_divide_fusion
  83.2 0.2 convolution_bitcast_fusion.1
  83.3 0.2 fusion.110
  83.5 0.3 fusion.1
  83.9 8.8 %all_to_all.36 = bf16[16,2,4,128]{3,1,2,0:T(2,128)(2,1)S(1)} all-to-all(bf16[16,2,4,128]{3,1,2,0:T(2,128)(2,1)S(1)} %copy.112), channel_id=1, replica_groups=mesh['mem'=8,'lat'=4] {'mem'}, dimensions={0} | all-to-all | bytes 65536 | tf_op jit(solution)/shard_map/all_to_all | solution.py:168
  92.7 0.6 all_to_all.33
  (94 shorter events, 3.4 us)
Async XLA Ops:
  0.8 6.5 %copy-start = (f32[2,4,1024]{2,1,0:T(4,128)S(1)}, f32[2,4,1024]{2,1,0:T(4,128)}, u32[]{:S(2)}) copy-start(f32[2,4,1024]{2,1,0:T(4,128)} %param.9) | copy-start | bytes 98308
  0.8 6.5 %copy-start.1 = (s32[1,256]{1,0:T(1,128)S(1)}, s32[1,256]{1,0:T(1,128)}, u32[]{:S(2)}) copy-start(s32[1,256]{1,0:T(1,128)} %param.10) | copy-start | bytes 3076
  0.8 10.1 %collective-permute-start = (f32[4,1,1024]{2,0,1:T(4,128)S(1)}, f32[4,1,1024]{2,0,1:T(4,128)S(1)}, u32[]{:S(2)}, u32[]{:S(2)}) collective-permute-start(f32[4,1,1024]{2,0,1:T(4,128)S(1)} %get-tuple-element.17), channel_id=1, source_target_pairs={{0,1},{1,2},{2,3},{4,5},{5,6},{6,7},{8,9},{9,10},{10,11},{12,13},{... | collective-permute-start | bytes 49160 | tf_op jit(solution)/shard_map/ppermute | solution.py:23
  5.4 5.6 %collective-permute-start.1 = (f32[4,1,1024]{2,0,1:T(4,128)S(1)}, f32[4,1,1024]{2,0,1:T(4,128)S(1)}, u32[]{:S(2)}, u32[]{:S(2)}) collective-permute-start(f32[4,1,1024]{2,0,1:T(4,128)S(1)} %get-tuple-element.18), channel_id=1, source_target_pairs={{1,0},{2,1},{3,2},{5,4},{6,5},{7,6},{9,8},{10,9},{11,10},{13,12},{... | collective-permute-start | bytes 49160 | tf_op jit(solution)/shard_map/ppermute | solution.py:25
  7.3 0.7 copy-start.2
  8.1 0.7 copy-start.6
  8.7 0.7 copy-start.7
  9.5 0.7 copy-start.5
  10.2 0.7 copy-start.8
  11.1 5.6 %collective-permute-start.2 = (f32[4,1,1024]{2,0,1:T(4,128)S(1)}, f32[4,1,1024]{2,0,1:T(4,128)S(1)}, u32[]{:S(2)}, u32[]{:S(2)}) collective-permute-start(f32[4,1,1024]{2,0,1:T(4,128)S(1)} %get-tuple-element.15), channel_id=1, source_target_pairs={{0,1},{1,2},{2,3},{4,5},{5,6},{6,7},{8,9},{9,10},{10,11},{12,13},{... | collective-permute-start | bytes 49160 | tf_op jit(solution)/shard_map/ppermute | solution.py:23
  14.8 5.1 %collective-permute-start.3 = (f32[4,1,1024]{2,0,1:T(4,128)S(1)}, f32[4,1,1024]{2,0,1:T(4,128)S(1)}, u32[]{:S(2)}, u32[]{:S(2)}) collective-permute-start(f32[4,1,1024]{2,0,1:T(4,128)S(1)} %get-tuple-element.16), channel_id=1, source_target_pairs={{1,0},{2,1},{3,2},{5,4},{6,5},{7,6},{9,8},{10,9},{11,10},{13,12},{... | collective-permute-start | bytes 49160 | tf_op jit(solution)/shard_map/ppermute | solution.py:25
  20.0 4.4 %collective-permute-start.4 = (f32[4,1,1024]{2,0,1:T(4,128)S(1)}, f32[4,1,1024]{2,0,1:T(4,128)S(1)}, u32[]{:S(2)}, u32[]{:S(2)}) collective-permute-start(f32[4,1,1024]{2,0,1:T(4,128)S(1)} %get-tuple-element.13), channel_id=1, source_target_pairs={{0,1},{1,2},{2,3},{4,5},{5,6},{6,7},{8,9},{9,10},{10,11},{12,13},{... | collective-permute-start | bytes 49160 | tf_op jit(solution)/shard_map/ppermute | solution.py:23
  21.9 5.1 %collective-permute-start.5 = (f32[4,1,1024]{2,0,1:T(4,128)S(1)}, f32[4,1,1024]{2,0,1:T(4,128)S(1)}, u32[]{:S(2)}, u32[]{:S(2)}) collective-permute-start(f32[4,1,1024]{2,0,1:T(4,128)S(1)} %get-tuple-element.14), channel_id=1, source_target_pairs={{1,0},{2,1},{3,2},{5,4},{6,5},{7,6},{9,8},{10,9},{11,10},{13,12},{... | collective-permute-start | bytes 49160 | tf_op jit(solution)/shard_map/ppermute | solution.py:25
  27.2 12.6 %collective-permute-start.6 = (f32[4,1,1024]{2,0,1:T(4,128)S(1)}, f32[4,1,1024]{2,0,1:T(4,128)S(1)}, u32[]{:S(2)}, u32[]{:S(2)}) collective-permute-start(f32[4,1,1024]{2,0,1:T(4,128)S(1)} %get-tuple-element.11), channel_id=1, source_target_pairs={{0,1},{1,2},{2,3},{4,5},{5,6},{6,7},{8,9},{9,10},{10,11},{12,13},{... | collective-permute-start | bytes 49160 | tf_op jit(solution)/shard_map/ppermute | solution.py:23
  29.1 10.7 %collective-permute-start.7 = (f32[4,1,1024]{2,0,1:T(4,128)S(1)}, f32[4,1,1024]{2,0,1:T(4,128)S(1)}, u32[]{:S(2)}, u32[]{:S(2)}) collective-permute-start(f32[4,1,1024]{2,0,1:T(4,128)S(1)} %get-tuple-element.12), channel_id=1, source_target_pairs={{1,0},{2,1},{3,2},{5,4},{6,5},{7,6},{9,8},{10,9},{11,10},{13,12},{... | collective-permute-start | bytes 49160 | tf_op jit(solution)/shard_map/ppermute | solution.py:25
  43.3 11.2 %all-to-all-start = ((bf16[8,2,1024]{2,1,0:T(2,128)(2,1)}), bf16[8,2,1024]{2,1,0:T(2,128)(2,1)S(1)}, u32[]{:S(2)}, u32[]{:S(2)}) async-start(bf16[8,2,1024]{2,1,0:T(2,128)(2,1)} %reshape.227), calls=%async_computation | async-start | bytes 65536 | tf_op jit(solution)/shard_map/all_to_all | solution.py:143
  59.2 0.7 copy-start.4
  59.2 0.7 copy-start.3
  60.0 3.7 %collective-permute-start.8 = (f32[1,1,20,256]{3,2,1,0:T(8,128)S(1)}, f32[1,1,20,256]{3,2,1,0:T(8,128)S(1)}, u32[]{:S(2)}, u32[]{:S(2)}) collective-permute-start(f32[1,1,20,256]{3,2,1,0:T(8,128)S(1)} %bitcast.132), channel_id=1, source_target_pairs={{0,4},{4,8},{8,12},{12,16},{16,20},{20,24},{24,28},{1,5},{5,9},{9,... | collective-permute-start | bytes 61448 | tf_op jit(solution)/shard_map/ppermute | solution.py:23
  62.3 4.6 %collective-permute-start.9 = (f32[1,1,20,256]{3,2,1,0:T(8,128)S(1)}, f32[1,1,20,256]{3,2,1,0:T(8,128)S(1)}, u32[]{:S(2)}, u32[]{:S(2)}) collective-permute-start(f32[1,1,20,256]{3,2,1,0:T(8,128)S(1)} %bitcast.133), channel_id=1, source_target_pairs={{4,0},{8,4},{12,8},{16,12},{20,16},{24,20},{28,24},{5,1},{9,5},{13... | collective-permute-start | bytes 61448 | tf_op jit(solution)/shard_map/ppermute | solution.py:25
  66.9 7.7 %collective-permute-start.10 = (f32[1,3,20,256]{3,0,2,1:T(1,128)S(1)}, f32[1,3,20,256]{3,0,2,1:T(1,128)S(1)}, u32[]{:S(2)}, u32[]{:S(2)}) collective-permute-start(f32[1,3,20,256]{3,0,2,1:T(1,128)S(1)} %copy_dynamic-update-slice_fusion), channel_id=1, source_target_pairs={{0,1},{1,2},{2,3},{4,5},{5,6},{6,7},{8,9},{9,10},{10,11},{12,13},{... | collective-permute-start | bytes 184328 | tf_op jit(solution)/shard_map/ppermute | solution.py:23
  72.6 5.5 %collective-permute-start.11 = (f32[1,3,20,256]{3,0,2,1:T(1,128)S(1)}, f32[1,3,20,256]{3,0,2,1:T(1,128)S(1)}, u32[]{:S(2)}, u32[]{:S(2)}) collective-permute-start(f32[1,3,20,256]{3,0,2,1:T(1,128)S(1)} %copy_dynamic-update-slice_fusion), channel_id=1, source_target_pairs={{1,0},{2,1},{3,2},{5,4},{6,5},{7,6},{9,8},{10,9},{11,10},{13,12},{... | collective-permute-start | bytes 184328 | tf_op jit(solution)/shard_map/ppermute | solution.py:25
where the time goes:
time: 94 us; the launch traced here: 93.3 us
  starting transfers between devices  37.4 us (40%)
  local copies, waits for them, and re-layouts  21 us (22%)
  waiting for transfers between devices  18.1 us (19%)
  blocking collectives  8.78 us (9%)
  matrix products  5.2 us (6%)
  other arithmetic  2.15 us (2%)
    ppermute x6, starting transfers between devices, with_halo(): lax.ppermute(tail, axis, [(i, (i + 1) % count) for i in range(ends)])  20 us
    unnamed x28, local copies, waits for them, and re-layouts  16.8 us
    ppermute x6, waiting for transfers between devices, with_halo(): lax.ppermute(head, axis, [((i + 1) % count, i) for i in range(ends)])  12.4 us
    ppermute x6, starting transfers between devices, with_halo(): lax.ppermute(head, axis, [((i + 1) % count, i) for i in range(ends)])  11.8 us
    all_to_all x1, blocking collectives, on_device(): lax.all_to_all(updated, 'mem', split_axis=0, concat_axis=3, tiled=True)  8.78 us
    all_to_all x1, waiting for transfers between devices, on_device(): lax.all_to_all(predict_advance, 'mem', split_axis=3, concat_axis=0, tiled...  5.62 us
    all_to_all x1, starting transfers between devices, on_device(): lax.all_to_all(predict_advance, 'mem', split_axis=3, concat_axis=0, tiled...  5.55 us
  transfers between devices with their start and end apart: 13, of which 5 were waited for; matrix products, arithmetic and copies ran while one was open for 9% of the time, Pallas kernels for 0%

commit v1 on v0

--- a/solution.py
+++ b/solution.py
@@ -10,6 +10,29 @@
 LOC_COLS = 64
 KAPPA = (0.025, 0.0125)
 HIGHEST = lax.Precision.HIGHEST
+
+
+def cut_along(x, dim, count):
+    before, after = (x.shape[:dim], x.shape[dim + 1 :])
+    return jnp.moveaxis(x.reshape(*before, count, -1, *after), dim, 0)
+
+
+def laid_out(tiles, dim):
+    tiles = jnp.moveaxis(tiles, 0, dim)
+    shape = tiles.shape
+    return tiles.reshape(*shape[:dim], shape[dim] * shape[dim + 1], *shape[dim + 2 :])
+
+
+def exchange_directly(shard, axis, split_dim, concat_dim):
+    count, index = (lax.axis_size(axis), lax.axis_index(axis))
+    parts = cut_along(shard, split_dim, count)
+    out = parts
+    for step in range(1, count):
+        target, source = ((index + step) % count, (index - step) % count)
+        sent = lax.dynamic_index_in_dim(parts, target, 0)
+        other = lax.ppermute(sent, axis, [(i, (i + step) % count) for i in range(count)])
+        out = lax.dynamic_update_slice_in_dim(out, other, source, axis=0)
+    return laid_out(out, concat_dim)
 
 
 def with_halo(cells, sides, width):
@@ -140,7 +163,7 @@
         ],
         axis=0,
     )
-    mesh_patches = lax.all_to_all(predict_advance, "mem", split_axis=3, concat_axis=0, tiled=True)
+    mesh_patches = exchange_directly(predict_advance, "mem", 3, 0)
     sample_realizations = mesh_patches.shape[0]
     own_obs = jnp.take(mesh_patches[:, 0].reshape(sample_realizations, -1), cells, axis=1).astype(
         jnp.float32

time: 94 us -> 86.3 us (0.918)
  the two profiles are of different devices: /device:TPU:1 before, /device:TPU:2 now
where the time goes in v1:
time: 86.3 us; the launch traced here: 85.6 us
  starting transfers between devices  43.5 us (50%)
  local copies, waits for them, and re-layouts  13.3 us (15%)
  blocking collectives  11.7 us (14%)
  waiting for transfers between devices  8.88 us (10%)
  matrix products  5.19 us (6%)
  other arithmetic  2.22 us (3%)
  between operations  0.87 us (1%)
    ppermute x6, starting transfers between devices, with_halo(): lax.ppermute(head, axis, [((i + 1) % count, i) for i in range(ends)])  16.1 us
    ppermute x6, starting transfers between devices, with_halo(): lax.ppermute(tail, axis, [(i, (i + 1) % count) for i in range(ends)])  15.1 us
    ppermute x7, starting transfers between devices, exchange_directly(): lax.ppermute(sent, axis, [(i, (i + step) % count) for i in range(count)])  12.3 us
    all_to_all x1, blocking collectives, on_device(): lax.all_to_all(updated, 'mem', split_axis=0, concat_axis=3, tiled=True)  11.7 us
    unnamed x28, local copies, waits for them, and re-layouts  10.7 us
    ppermute x6, waiting for transfers between devices, with_halo(): lax.ppermute(tail, axis, [(i, (i + 1) % count) for i in range(ends)])  4.75 us
    ppermute x6, waiting for transfers between devices, with_halo(): lax.ppermute(head, axis, [((i + 1) % count, i) for i in range(ends)])  4.1 us
  transfers between devices with their start and end apart: 19, of which 6 were waited for; matrix products, arithmetic and copies ran while one was open for 11% of the time, Pallas kernels for 0%

profile of v1, /device:TPU:2, one launch (start us, length us, event | category | flops | bytes accessed | tf_op | source)
XLA Modules:
  0.0 85.6 jit_solution(15083743646276781989)
XLA Ops:
  0.0 0.8 bitcast_convert_fusion
  0.8 1.9 %collective-permute-start.1 = (f32[4,1,1024]{2,1,0:T(1,128)S(1)}, f32[4,1,1024]{2,1,0:T(1,128)S(1)}, u32[]{:S(2)}, u32[]{:S(2)}) collective-permute-start(f32[4,1,1024]{2,1,0:T(1,128)S(1)} %get-tuple-element.17), channel_id=1, source_target_pairs={{1,0},{2,1},{3,2},{5,4},{6,5},{7,6},{9,8},{10,9},{11,10},{13,12},{... | collective-permute-start | bytes 49160 | tf_op jit(solution)/shard_map/ppermute | solution.py:48
  2.7 2.4 %collective-permute-start = (f32[4,1,1024]{2,1,0:T(1,128)S(1)}, f32[4,1,1024]{2,1,0:T(1,128)S(1)}, u32[]{:S(2)}, u32[]{:S(2)}) collective-permute-start(f32[4,1,1024]{2,1,0:T(1,128)S(1)} %get-tuple-element.18), channel_id=1, source_target_pairs={{0,1},{1,2},{2,3},{4,5},{5,6},{6,7},{8,9},{9,10},{10,11},{12,13},{... | collective-permute-start | bytes 49160 | tf_op jit(solution)/shard_map/ppermute | solution.py:46
  5.3 0.6 copy-done.7
  6.1 0.6 copy-done.6
  6.9 0.6 copy-done.9
  7.6 0.2 collective-permute-done
  8.0 1.9 %collective-permute-start.2 = (f32[4,1,1024]{2,1,0:T(1,128)S(1)}, f32[4,1,1024]{2,1,0:T(1,128)S(1)}, u32[]{:S(2)}, u32[]{:S(2)}) collective-permute-start(f32[4,1,1024]{2,1,0:T(1,128)S(1)} %get-tuple-element.15), channel_id=1, source_target_pairs={{0,1},{1,2},{2,3},{4,5},{5,6},{6,7},{8,9},{9,10},{10,11},{12,13},{... | collective-permute-start | bytes 49160 | tf_op jit(solution)/shard_map/ppermute | solution.py:46
  9.9 3.6 %collective-permute-start.3 = (f32[4,1,1024]{2,1,0:T(1,128)S(1)}, f32[4,1,1024]{2,1,0:T(1,128)S(1)}, u32[]{:S(2)}, u32[]{:S(2)}) collective-permute-start(f32[4,1,1024]{2,1,0:T(1,128)S(1)} %get-tuple-element.16), channel_id=1, source_target_pairs={{1,0},{2,1},{3,2},{5,4},{6,5},{7,6},{9,8},{10,9},{11,10},{13,12},{... | collective-permute-start | bytes 49160 | tf_op jit(solution)/shard_map/ppermute | solution.py:48
  13.6 1.4 %collective-permute-done.3 = f32[4,1,1024]{2,1,0:T(1,128)S(1)} collective-permute-done((f32[4,1,1024]{2,1,0:T(1,128)S(1)}, f32[4,1,1024]{2,1,0:T(1,128)S(1)}, u32[]{:S(2)}, u32[]{:S(2)}) %collective-permute-start.3) | collective-permute-done | bytes 16416 | tf_op jit(solution)/shard_map/ppermute | solution.py:48
  15.2 1.9 %collective-permute-start.4 = (f32[4,1,1024]{2,1,0:T(1,128)S(1)}, f32[4,1,1024]{2,1,0:T(1,128)S(1)}, u32[]{:S(2)}, u32[]{:S(2)}) collective-permute-start(f32[4,1,1024]{2,1,0:T(1,128)S(1)} %get-tuple-element.13), channel_id=1, source_target_pairs={{0,1},{1,2},{2,3},{4,5},{5,6},{6,7},{8,9},{9,10},{10,11},{12,13},{... | collective-permute-start | bytes 49160 | tf_op jit(solution)/shard_map/ppermute | solution.py:46
  17.1 3.6 %collective-permute-start.5 = (f32[4,1,1024]{2,1,0:T(1,128)S(1)}, f32[4,1,1024]{2,1,0:T(1,128)S(1)}, u32[]{:S(2)}, u32[]{:S(2)}) collective-permute-start(f32[4,1,1024]{2,1,0:T(1,128)S(1)} %get-tuple-element.14), channel_id=1, source_target_pairs={{1,0},{2,1},{3,2},{5,4},{6,5},{7,6},{9,8},{10,9},{11,10},{13,12},{... | collective-permute-start | bytes 49160 | tf_op jit(solution)/shard_map/ppermute | solution.py:48
  20.8 1.4 %collective-permute-done.5 = f32[4,1,1024]{2,1,0:T(1,128)S(1)} collective-permute-done((f32[4,1,1024]{2,1,0:T(1,128)S(1)}, f32[4,1,1024]{2,1,0:T(1,128)S(1)}, u32[]{:S(2)}, u32[]{:S(2)}) %collective-permute-start.5) | collective-permute-done | bytes 16416 | tf_op jit(solution)/shard_map/ppermute | solution.py:48
  22.4 1.9 %collective-permute-start.6 = (f32[4,1,1024]{2,1,0:T(1,128)S(1)}, f32[4,1,1024]{2,1,0:T(1,128)S(1)}, u32[]{:S(2)}, u32[]{:S(2)}) collective-permute-start(f32[4,1,1024]{2,1,0:T(1,128)S(1)} %get-tuple-element.11), channel_id=1, source_target_pairs={{0,1},{1,2},{2,3},{4,5},{5,6},{6,7},{8,9},{9,10},{10,11},{12,13},{... | collective-permute-start | bytes 49160 | tf_op jit(solution)/shard_map/ppermute | solution.py:46
  24.3 3.6 %collective-permute-start.7 = (f32[4,1,1024]{2,1,0:T(1,128)S(1)}, f32[4,1,1024]{2,1,0:T(1,128)S(1)}, u32[]{:S(2)}, u32[]{:S(2)}) collective-permute-start(f32[4,1,1024]{2,1,0:T(1,128)S(1)} %get-tuple-element.12), channel_id=1, source_target_pairs={{1,0},{2,1},{3,2},{5,4},{6,5},{7,6},{9,8},{10,9},{11,10},{13,12},{... | collective-permute-start | bytes 49160 | tf_op jit(solution)/shard_map/ppermute | solution.py:48
  28.1 1.3 %collective-permute-done.7 = f32[4,1,1024]{2,1,0:T(1,128)S(1)} collective-permute-done((f32[4,1,1024]{2,1,0:T(1,128)S(1)}, f32[4,1,1024]{2,1,0:T(1,128)S(1)}, u32[]{:S(2)}, u32[]{:S(2)}) %collective-permute-start.7) | collective-permute-done | bytes 16416 | tf_op jit(solution)/shard_map/ppermute | solution.py:48
  29.4 0.2 fusion.64
  29.7 1.6 %collective-permute-start.9 = (bf16[1,2,2,4,128]{4,0,3,2,1:T(2,128)(2,1)S(1)}, bf16[1,2,2,4,128]{4,0,3,2,1:T(2,128)(2,1)S(1)}, u32[]{:S(2)}, u32[]{:S(2)}) collective-permute-start(bf16[1,2,2,4,128]{4,0,3,2,1:T(2,128)(2,1)S(1)} %get-tuple-element.28), channel_id=1, source_target_pairs={{0,8},{4,12},{8,16},{12,20},{16,24},{20,28},{24,0},{28,4},{1,9},{5... | collective-permute-start | bytes 12296 | tf_op jit(solution)/shard_map/ppermute | solution.py:33
  31.3 1.5 %collective-permute-start.8 = (bf16[1,2,2,4,128]{4,0,3,2,1:T(2,128)(2,1)S(1)}, bf16[1,2,2,4,128]{4,0,3,2,1:T(2,128)(2,1)S(1)}, u32[]{:S(2)}, u32[]{:S(2)}) collective-permute-start(bf16[1,2,2,4,128]{4,0,3,2,1:T(2,128)(2,1)S(1)} %get-tuple-element.29), channel_id=1, source_target_pairs={{0,4},{4,8},{8,12},{12,16},{16,20},{20,24},{24,28},{28,0},{1,5},{5... | collective-permute-start | bytes 12296 | tf_op jit(solution)/shard_map/ppermute | solution.py:33
  32.8 2.2 %collective-permute-start.12 = (bf16[1,2,2,4,128]{4,0,3,2,1:T(2,128)(2,1)S(1)}, bf16[1,2,2,4,128]{4,0,3,2,1:T(2,128)(2,1)S(1)}, u32[]{:S(2)}, u32[]{:S(2)}) collective-permute-start(bf16[1,2,2,4,128]{4,0,3,2,1:T(2,128)(2,1)S(1)} %get-tuple-element.25), channel_id=1, source_target_pairs={{0,20},{4,24},{8,28},{12,0},{16,4},{20,8},{24,12},{28,16},{1,21},{... | collective-permute-start | bytes 12296 | tf_op jit(solution)/shard_map/ppermute | solution.py:33
  35.0 0.7 collective-permute-start.10
  35.8 2.6 %collective-permute-start.11 = (bf16[1,2,2,4,128]{4,0,3,2,1:T(2,128)(2,1)S(1)}, bf16[1,2,2,4,128]{4,0,3,2,1:T(2,128)(2,1)S(1)}, u32[]{:S(2)}, u32[]{:S(2)}) collective-permute-start(bf16[1,2,2,4,128]{4,0,3,2,1:T(2,128)(2,1)S(1)} %get-tuple-element.26), channel_id=1, source_target_pairs={{0,16},{4,20},{8,24},{12,28},{16,0},{20,4},{24,8},{28,12},{1,17},{... | collective-permute-start | bytes 12296 | tf_op jit(solution)/shard_map/ppermute | solution.py:33
  38.4 1.5 %collective-permute-start.13 = (bf16[1,2,2,4,128]{4,0,3,2,1:T(2,128)(2,1)S(1)}, bf16[1,2,2,4,128]{4,0,3,2,1:T(2,128)(2,1)S(1)}, u32[]{:S(2)}, u32[]{:S(2)}) collective-permute-start(bf16[1,2,2,4,128]{4,0,3,2,1:T(2,128)(2,1)S(1)} %get-tuple-element.24), channel_id=1, source_target_pairs={{0,24},{4,28},{8,0},{12,4},{16,8},{20,12},{24,16},{28,20},{1,25},{... | collective-permute-start | bytes 12296 | tf_op jit(solution)/shard_map/ppermute | solution.py:33
  39.8 2.2 %collective-permute-start.14 = (bf16[1,2,2,4,128]{4,0,3,2,1:T(2,128)(2,1)S(1)}, bf16[1,2,2,4,128]{4,0,3,2,1:T(2,128)(2,1)S(1)}, u32[]{:S(2)}, u32[]{:S(2)}) collective-permute-start(bf16[1,2,2,4,128]{4,0,3,2,1:T(2,128)(2,1)S(1)} %get-tuple-element.23), channel_id=1, source_target_pairs={{0,28},{4,0},{8,4},{12,8},{16,12},{20,16},{24,20},{28,24},{1,29},{... | collective-permute-start | bytes 12296 | tf_op jit(solution)/shard_map/ppermute | solution.py:33
  42.0 8.1 %scatter_custom_fusion = f32[5120]{0:T(1024)S(1)} fusion(s32[2048]{0:T(1024)S(1)} %bitcast.152, f32[2048]{0:T(1024)S(1)} %bitcast.153, f32[]{:T(128)} %constant.165.clone.1), kind=kCustom, calls=%fused_computation.137 | custom fusion | bytes 20484
  50.9 0.9 %gather_fusion = bf16[256,16]{1,0:T(8,128)(2,1)S(1)} fusion(bf16[16,512]{0,1:T(8,128)(2,1)S(1)} %bitcast.140, s32[1024]{0:T(1024)S(1)} %pad_clamp_fusion), kind=kCustom, calls=%fused_computation | custom fusion | bytes 17408 | tf_op jit(solution)/shard_map/jit(_take)/gather | solution.py:168
  51.9 0.6 copy-done.5
  52.6 1.3 %collective-permute-start.16 = (f32[1,1,20,256]{3,2,1,0:T(8,128)S(1)}, f32[1,1,20,256]{3,2,1,0:T(8,128)S(1)}, u32[]{:S(2)}, u32[]{:S(2)}) collective-permute-start(f32[1,1,20,256]{3,2,1,0:T(8,128)S(1)} %bitcast.141), channel_id=1, source_target_pairs={{4,0},{8,4},{12,8},{16,12},{20,16},{24,20},{28,24},{5,1},{9,5},{13... | collective-permute-start | bytes 61448 | tf_op jit(solution)/shard_map/ppermute | solution.py:48
  53.9 4.5 %collective-permute-start.15 = (f32[1,1,20,256]{3,2,1,0:T(8,128)S(1)}, f32[1,1,20,256]{3,2,1,0:T(8,128)S(1)}, u32[]{:S(2)}, u32[]{:S(2)}) collective-permute-start(f32[1,1,20,256]{3,2,1,0:T(8,128)S(1)} %bitcast.142), channel_id=1, source_target_pairs={{0,4},{4,8},{8,12},{12,16},{16,20},{20,24},{24,28},{1,5},{5,9},{9,... | collective-permute-start | bytes 61448 | tf_op jit(solution)/shard_map/ppermute | solution.py:46
  58.5 1.5 %collective-permute-done.15 = f32[1,1,20,256]{3,2,1,0:T(8,128)S(1)} collective-permute-done((f32[1,1,20,256]{3,2,1,0:T(8,128)S(1)}, f32[1,1,20,256]{3,2,1,0:T(8,128)S(1)}, u32[]{:S(2)}, u32[]{:S(2)}) %collective-permute-start.15) | collective-permute-done | bytes 20512 | tf_op jit(solution)/shard_map/ppermute | solution.py:46
  60.1 1.9 %collective-permute-start.18 = (f32[1,3,20,256]{3,0,2,1:T(1,128)S(1)}, f32[1,3,20,256]{3,0,2,1:T(1,128)S(1)}, u32[]{:S(2)}, u32[]{:S(2)}) collective-permute-start(f32[1,3,20,256]{3,0,2,1:T(1,128)S(1)} %copy_dynamic-update-slice_fusion), channel_id=1, source_target_pairs={{1,0},{2,1},{3,2},{5,4},{6,5},{7,6},{9,8},{10,9},{11,10},{13,12},{... | collective-permute-start | bytes 184328 | tf_op jit(solution)/shard_map/ppermute | solution.py:48
  62.0 2.4 %collective-permute-start.17 = (f32[1,3,20,256]{3,0,2,1:T(1,128)S(1)}, f32[1,3,20,256]{3,0,2,1:T(1,128)S(1)}, u32[]{:S(2)}, u32[]{:S(2)}) collective-permute-start(f32[1,3,20,256]{3,0,2,1:T(1,128)S(1)} %copy_dynamic-update-slice_fusion), channel_id=1, source_target_pairs={{0,1},{1,2},{2,3},{4,5},{5,6},{6,7},{8,9},{9,10},{10,11},{12,13},{... | collective-permute-start | bytes 184328 | tf_op jit(solution)/shard_map/ppermute | solution.py:46
  64.5 3.0 %collective-permute-done.17 = f32[1,3,20,256]{3,0,2,1:T(1,128)S(1)} collective-permute-done((f32[1,3,20,256]{3,0,2,1:T(1,128)S(1)}, f32[1,3,20,256]{3,0,2,1:T(1,128)S(1)}, u32[]{:S(2)}, u32[]{:S(2)}) %collective-permute-start.17) | collective-permute-done | bytes 61472 | tf_op jit(solution)/shard_map/ppermute | solution.py:46
  67.8 1.3 %abs_reduce_fusion = (f32[4,16]{1,0:T(4,128)S(1)}, f32[4,16,16]{1,2,0:T(8,128)S(1)}) fusion(f32[16,1280]{1,0:T(8,128)S(1)} %slice_subtract_fusion, f32[4,1280]{1,0:T(4,128)S(1)} %multiply_multiply_fusion), kind=kOutput, calls=%fused_computation.107 | convolution fusion | flops 15812544 | bytes 106752 | tf_op jit(solution)/shard_map/rek,fk->ref/dot_general | solution.py:116
  69.2 0.3 fusion.7
  69.5 0.3 fusion.94
  70.0 0.2 fusion.6
  70.5 0.2 fusion.5
  71.0 0.2 fusion.4
  71.2 0.2 fusion.104
  71.5 0.2 fusion.3
  72.0 0.2 fusion.69
  72.2 0.2 fusion.2
  72.6 0.2 convolution_bitcast_fusion.1
  72.7 0.2 fusion.107
  72.9 0.3 fusion.1
  73.3 11.7 %all_to_all.18 = bf16[16,2,4,128]{3,1,2,0:T(2,128)(2,1)S(1)} all-to-all(bf16[16,2,4,128]{3,1,2,0:T(2,128)(2,1)S(1)} %copy.75), channel_id=1, replica_groups=mesh['mem'=8,'lat'=4] {'mem'}, dimensions={0} | all-to-all | bytes 65536 | tf_op jit(solution)/shard_map/all_to_all | solution.py:191
  85.0 0.6 all_to_all.16
  (112 shorter events, 4.1 us)
Async XLA Ops:
  0.8 4.4 %copy-start.2 = (s32[1,256]{1,0:T(1,128)S(1)}, s32[1,256]{1,0:T(1,128)}, u32[]{:S(2)}) copy-start(s32[1,256]{1,0:T(1,128)} %param.10) | copy-start | bytes 3076
  0.8 4.4 %copy-start.3 = (s32[4,1,512]{2,1,0:T(1,128)S(1)}, s32[4,1,512]{2,1,0:T(1,128)}, u32[]{:S(2)}) copy-start(s32[4,1,512]{2,1,0:T(1,128)} %param.13) | copy-start | bytes 24580
  0.8 6.8 %collective-permute-start.1 = (f32[4,1,1024]{2,1,0:T(1,128)S(1)}, f32[4,1,1024]{2,1,0:T(1,128)S(1)}, u32[]{:S(2)}, u32[]{:S(2)}) collective-permute-start(f32[4,1,1024]{2,1,0:T(1,128)S(1)} %get-tuple-element.17), channel_id=1, source_target_pairs={{1,0},{2,1},{3,2},{5,4},{6,5},{7,6},{9,8},{10,9},{11,10},{13,12},{... | collective-permute-start | bytes 49160 | tf_op jit(solution)/shard_map/ppermute | solution.py:48
  2.7 5.1 %collective-permute-start = (f32[4,1,1024]{2,1,0:T(1,128)S(1)}, f32[4,1,1024]{2,1,0:T(1,128)S(1)}, u32[]{:S(2)}, u32[]{:S(2)}) collective-permute-start(f32[4,1,1024]{2,1,0:T(1,128)S(1)} %get-tuple-element.18), channel_id=1, source_target_pairs={{0,1},{1,2},{2,3},{4,5},{5,6},{6,7},{8,9},{9,10},{10,11},{12,13},{... | collective-permute-start | bytes 49160 | tf_op jit(solution)/shard_map/ppermute | solution.py:46
  5.2 0.7 copy-start.7
  5.2 0.8 copy-start.8
  5.3 1.6 %copy-start.1 = (f32[2,4,1024]{2,1,0:T(4,128)S(1)}, f32[2,4,1024]{2,1,0:T(4,128)}, u32[]{:S(2)}) copy-start(f32[2,4,1024]{2,1,0:T(4,128)} %param.9) | copy-start | bytes 98308
  6.1 0.7 copy-start.6
  6.8 0.7 copy-start.9
  6.8 1.0 %copy-start = (bf16[2,2,4,1024]{3,2,1,0:T(4,128)(2,1)S(1)}, bf16[2,2,4,1024]{3,2,1,0:T(4,128)(2,1)}, u32[]{:S(2)}) copy-start(bf16[2,2,4,1024]{3,2,1,0:T(4,128)(2,1)} %param.8) | copy-start | bytes 98308
  8.0 5.6 %collective-permute-start.2 = (f32[4,1,1024]{2,1,0:T(1,128)S(1)}, f32[4,1,1024]{2,1,0:T(1,128)S(1)}, u32[]{:S(2)}, u32[]{:S(2)}) collective-permute-start(f32[4,1,1024]{2,1,0:T(1,128)S(1)} %get-tuple-element.15), channel_id=1, source_target_pairs={{0,1},{1,2},{2,3},{4,5},{5,6},{6,7},{8,9},{9,10},{10,11},{12,13},{... | collective-permute-start | bytes 49160 | tf_op jit(solution)/shard_map/ppermute | solution.py:46
  9.9 5.1 %collective-permute-start.3 = (f32[4,1,1024]{2,1,0:T(1,128)S(1)}, f32[4,1,1024]{2,1,0:T(1,128)S(1)}, u32[]{:S(2)}, u32[]{:S(2)}) collective-permute-start(f32[4,1,1024]{2,1,0:T(1,128)S(1)} %get-tuple-element.16), channel_id=1, source_target_pairs={{1,0},{2,1},{3,2},{5,4},{6,5},{7,6},{9,8},{10,9},{11,10},{13,12},{... | collective-permute-start | bytes 49160 | tf_op jit(solution)/shard_map/ppermute | solution.py:48
  15.2 5.6 %collective-permute-start.4 = (f32[4,1,1024]{2,1,0:T(1,128)S(1)}, f32[4,1,1024]{2,1,0:T(1,128)S(1)}, u32[]{:S(2)}, u32[]{:S(2)}) collective-permute-start(f32[4,1,1024]{2,1,0:T(1,128)S(1)} %get-tuple-element.13), channel_id=1, source_target_pairs={{0,1},{1,2},{2,3},{4,5},{5,6},{6,7},{8,9},{9,10},{10,11},{12,13},{... | collective-permute-start | bytes 49160 | tf_op jit(solution)/shard_map/ppermute | solution.py:46
  17.1 5.1 %collective-permute-start.5 = (f32[4,1,1024]{2,1,0:T(1,128)S(1)}, f32[4,1,1024]{2,1,0:T(1,128)S(1)}, u32[]{:S(2)}, u32[]{:S(2)}) collective-permute-start(f32[4,1,1024]{2,1,0:T(1,128)S(1)} %get-tuple-element.14), channel_id=1, source_target_pairs={{1,0},{2,1},{3,2},{5,4},{6,5},{7,6},{9,8},{10,9},{11,10},{13,12},{... | collective-permute-start | bytes 49160 | tf_op jit(solution)/shard_map/ppermute | solution.py:48
  22.4 5.7 %collective-permute-start.6 = (f32[4,1,1024]{2,1,0:T(1,128)S(1)}, f32[4,1,1024]{2,1,0:T(1,128)S(1)}, u32[]{:S(2)}, u32[]{:S(2)}) collective-permute-start(f32[4,1,1024]{2,1,0:T(1,128)S(1)} %get-tuple-element.11), channel_id=1, source_target_pairs={{0,1},{1,2},{2,3},{4,5},{5,6},{6,7},{8,9},{9,10},{10,11},{12,13},{... | collective-permute-start | bytes 49160 | tf_op jit(solution)/shard_map/ppermute | solution.py:46
  24.3 5.1 %collective-permute-start.7 = (f32[4,1,1024]{2,1,0:T(1,128)S(1)}, f32[4,1,1024]{2,1,0:T(1,128)S(1)}, u32[]{:S(2)}, u32[]{:S(2)}) collective-permute-start(f32[4,1,1024]{2,1,0:T(1,128)S(1)} %get-tuple-element.12), channel_id=1, source_target_pairs={{1,0},{2,1},{3,2},{5,4},{6,5},{7,6},{9,8},{10,9},{11,10},{13,12},{... | collective-permute-start | bytes 49160 | tf_op jit(solution)/shard_map/ppermute | solution.py:48
  29.7 8.7 %collective-permute-start.9 = (bf16[1,2,2,4,128]{4,0,3,2,1:T(2,128)(2,1)S(1)}, bf16[1,2,2,4,128]{4,0,3,2,1:T(2,128)(2,1)S(1)}, u32[]{:S(2)}, u32[]{:S(2)}) collective-permute-start(bf16[1,2,2,4,128]{4,0,3,2,1:T(2,128)(2,1)S(1)} %get-tuple-element.28), channel_id=1, source_target_pairs={{0,8},{4,12},{8,16},{12,20},{16,24},{20,28},{24,0},{28,4},{1,9},{5... | collective-permute-start | bytes 12296 | tf_op jit(solution)/shard_map/ppermute | solution.py:33
  31.3 8.5 %collective-permute-start.8 = (bf16[1,2,2,4,128]{4,0,3,2,1:T(2,128)(2,1)S(1)}, bf16[1,2,2,4,128]{4,0,3,2,1:T(2,128)(2,1)S(1)}, u32[]{:S(2)}, u32[]{:S(2)}) collective-permute-start(bf16[1,2,2,4,128]{4,0,3,2,1:T(2,128)(2,1)S(1)} %get-tuple-element.29), channel_id=1, source_target_pairs={{0,4},{4,8},{8,12},{12,16},{16,20},{20,24},{24,28},{28,0},{1,5},{5... | collective-permute-start | bytes 12296 | tf_op jit(solution)/shard_map/ppermute | solution.py:33
  32.8 17.6 %collective-permute-start.12 = (bf16[1,2,2,4,128]{4,0,3,2,1:T(2,128)(2,1)S(1)}, bf16[1,2,2,4,128]{4,0,3,2,1:T(2,128)(2,1)S(1)}, u32[]{:S(2)}, u32[]{:S(2)}) collective-permute-start(bf16[1,2,2,4,128]{4,0,3,2,1:T(2,128)(2,1)S(1)} %get-tuple-element.25), channel_id=1, source_target_pairs={{0,20},{4,24},{8,28},{12,0},{16,4},{20,8},{24,12},{28,16},{1,21},{... | collective-permute-start | bytes 12296 | tf_op jit(solution)/shard_map/ppermute | solution.py:33
  35.0 15.3 %collective-permute-start.10 = (bf16[1,2,2,4,128]{4,0,3,2,1:T(2,128)(2,1)S(1)}, bf16[1,2,2,4,128]{4,0,3,2,1:T(2,128)(2,1)S(1)}, u32[]{:S(2)}, u32[]{:S(2)}) collective-permute-start(bf16[1,2,2,4,128]{4,0,3,2,1:T(2,128)(2,1)S(1)} %get-tuple-element.27), channel_id=1, source_target_pairs={{0,12},{4,16},{8,20},{12,24},{16,28},{20,0},{24,4},{28,8},{1,13},{... | collective-permute-start | bytes 12296 | tf_op jit(solution)/shard_map/ppermute | solution.py:33
  35.8 14.6 %collective-permute-start.11 = (bf16[1,2,2,4,128]{4,0,3,2,1:T(2,128)(2,1)S(1)}, bf16[1,2,2,4,128]{4,0,3,2,1:T(2,128)(2,1)S(1)}, u32[]{:S(2)}, u32[]{:S(2)}) collective-permute-start(bf16[1,2,2,4,128]{4,0,3,2,1:T(2,128)(2,1)S(1)} %get-tuple-element.26), channel_id=1, source_target_pairs={{0,16},{4,20},{8,24},{12,28},{16,0},{20,4},{24,8},{28,12},{1,17},{... | collective-permute-start | bytes 12296 | tf_op jit(solution)/shard_map/ppermute | solution.py:33
  38.4 12.2 %collective-permute-start.13 = (bf16[1,2,2,4,128]{4,0,3,2,1:T(2,128)(2,1)S(1)}, bf16[1,2,2,4,128]{4,0,3,2,1:T(2,128)(2,1)S(1)}, u32[]{:S(2)}, u32[]{:S(2)}) collective-permute-start(bf16[1,2,2,4,128]{4,0,3,2,1:T(2,128)(2,1)S(1)} %get-tuple-element.24), channel_id=1, source_target_pairs={{0,24},{4,28},{8,0},{12,4},{16,8},{20,12},{24,16},{28,20},{1,25},{... | collective-permute-start | bytes 12296 | tf_op jit(solution)/shard_map/ppermute | solution.py:33
  39.8 10.8 %collective-permute-start.14 = (bf16[1,2,2,4,128]{4,0,3,2,1:T(2,128)(2,1)S(1)}, bf16[1,2,2,4,128]{4,0,3,2,1:T(2,128)(2,1)S(1)}, u32[]{:S(2)}, u32[]{:S(2)}) collective-permute-start(bf16[1,2,2,4,128]{4,0,3,2,1:T(2,128)(2,1)S(1)} %get-tuple-element.23), channel_id=1, source_target_pairs={{0,28},{4,0},{8,4},{12,8},{16,12},{20,16},{24,20},{28,24},{1,29},{... | collective-permute-start | bytes 12296 | tf_op jit(solution)/shard_map/ppermute | solution.py:33
  51.8 0.7 copy-start.5
  51.9 0.7 copy-start.4
  52.6 7.4 %collective-permute-start.16 = (f32[1,1,20,256]{3,2,1,0:T(8,128)S(1)}, f32[1,1,20,256]{3,2,1,0:T(8,128)S(1)}, u32[]{:S(2)}, u32[]{:S(2)}) collective-permute-start(f32[1,1,20,256]{3,2,1,0:T(8,128)S(1)} %bitcast.141), channel_id=1, source_target_pairs={{4,0},{8,4},{12,8},{16,12},{20,16},{24,20},{28,24},{5,1},{9,5},{13... | collective-permute-start | bytes 61448 | tf_op jit(solution)/shard_map/ppermute | solution.py:48
  53.9 6.1 %collective-permute-start.15 = (f32[1,1,20,256]{3,2,1,0:T(8,128)S(1)}, f32[1,1,20,256]{3,2,1,0:T(8,128)S(1)}, u32[]{:S(2)}, u32[]{:S(2)}) collective-permute-start(f32[1,1,20,256]{3,2,1,0:T(8,128)S(1)} %bitcast.142), channel_id=1, source_target_pairs={{0,4},{4,8},{8,12},{12,16},{16,20},{20,24},{24,28},{1,5},{5,9},{9,... | collective-permute-start | bytes 61448 | tf_op jit(solution)/shard_map/ppermute | solution.py:46
  60.1 4.4 %collective-permute-start.18 = (f32[1,3,20,256]{3,0,2,1:T(1,128)S(1)}, f32[1,3,20,256]{3,0,2,1:T(1,128)S(1)}, u32[]{:S(2)}, u32[]{:S(2)}) collective-permute-start(f32[1,3,20,256]{3,0,2,1:T(1,128)S(1)} %copy_dynamic-update-slice_fusion), channel_id=1, source_target_pairs={{1,0},{2,1},{3,2},{5,4},{6,5},{7,6},{9,8},{10,9},{11,10},{13,12},{... | collective-permute-start | bytes 184328 | tf_op jit(solution)/shard_map/ppermute | solution.py:48
  62.0 5.5 %collective-permute-start.17 = (f32[1,3,20,256]{3,0,2,1:T(1,128)S(1)}, f32[1,3,20,256]{3,0,2,1:T(1,128)S(1)}, u32[]{:S(2)}, u32[]{:S(2)}) collective-permute-start(f32[1,3,20,256]{3,0,2,1:T(1,128)S(1)} %copy_dynamic-update-slice_fusion), channel_id=1, source_target_pairs={{0,1},{1,2},{2,3},{4,5},{5,6},{6,7},{8,9},{9,10},{10,11},{12,13},{... | collective-permute-start | bytes 184328 | tf_op jit(solution)/shard_map/ppermute | solution.py:46
